TPU v7x, 32 devices: a whole 2x2x4 slice. The times are simulated.
32 devices in a mesh: row: 4 (over y, x), col: 8 (over z, core).
Axes of the slice: x: 2, y: 2, z: 4, core: 2. Of those that a mesh axis runs over, the one named last changes fastest.
Arguments:
- integrals: bfloat16 [2880, 23040], P('row', 'col'), may hold values from -0.0390625 to 0.0390625
- amplitudes: bfloat16 [23040, 256], P('col', 'row'), may hold values from -6 to 6
Outputs:
- ladder: bfloat16 [256, 2880], P('col', 'row')
All inputs are finite; a program needn't handle non-finite values.
Results may differ from a plain program's by a relative error of at most 0.001.
Values may be sent and summed in bfloat16 or wider, within the bound.
A program may use at most 64 MiB of HBM per device.

v0:
```python
import jax
import jax.numpy as jnp
from jax import lax
from jax.sharding import PartitionSpec as P


def per_device(integrals, amplitudes):
    columns = lax.axis_size("col")
    gathered = lax.all_gather(amplitudes, "row", axis=1, tiled=True)
    local_rows = integrals.shape[0]
    row_count = (local_rows + columns - 1) // columns
    padded_rows = row_count * columns
    padded = jnp.pad(integrals, ((0, padded_rows - local_rows), (0, 0)))
    totals = lax.psum_scatter(
        jnp.dot(padded, gathered, preferred_element_type=jnp.float32),
        "col",
        scatter_dimension=0,
        tiled=True,
    ).astype(jnp.bfloat16)
    regrouped = lax.all_to_all(totals, "col", split_axis=1, concat_axis=0, tiled=True)
    return regrouped[:local_rows].T


def solution(mesh):
    in_specs = (P("row", "col"), P("col", "row"))
    out_specs = P("col", "row")
    return jax.shard_map(
        per_device, mesh=mesh, in_specs=in_specs, out_specs=out_specs, check_vma=False
    )
```

profile of v0, /device:TPU:0, one launch (start us, length us, event | category | flops | bytes accessed | tf_op | source)
XLA Modules:
  0.0 86.1 jit_solution(9630065998873702536)
XLA Ops:
  6.5 0.0 all-gather.2.cloned.1.call-start
  6.5 0.7 all-gather.2.cloned.1.call-update
  7.3 0.0 copy-start
  7.3 35.0 %all-gather.2.cloned.1.call-done = bf16[2880,256]{0,1:T(8,128)(2,1)} async-done(((bf16[2880,64]{0,1:T(8,128)(2,1)}), bf16[2880,256]{0,1:T(8,128)(2,1)}) %all-gather.2.cloned.1.call-update) | async-done | bytes 1474576 | tf_op jit(solution)/shard_map/all_gather | solution.py:9
  42.2 4.0 %fusion.1 = f32[720,256]{1,0:T(8,128)S(1)} fusion(bf16[720,2880]{1,0:T(8,128)(2,1)} %param.2, bf16[2880,256]{0,1:T(8,128)(2,1)} %all-gather.2.cloned.1.call-done), kind=kOutput, calls=%fused_computation.1 | convolution fusion | flops 1061683200 | bytes 6359040 | tf_op jit(solution)/shard_map/dot_general | solution.py:15
  46.2 20.7 %fusion = f32[96,256]{1,0:T(8,128)S(1)} fusion(f32[720,256]{1,0:T(8,128)S(1)} %fusion.1), kind=kCustom, calls=%all-reduce-scatter | all-reduce-scatter fusion | flops 196609 | bytes 836096
  67.0 1.3 %collective-permute-start = (bf16[42,256]{1,0:T(8,128)(2,1)S(1)}, bf16[42,256]{1,0:T(8,128)(2,1)S(1)}, u32[]{:S(2)}, u32[]{:S(2)}) collective-permute-start(bf16[42,256]{1,0:T(8,128)(2,1)S(1)} %slice), channel_id=1, source_target_pairs={{0,1},{1,2},{2,3},{3,4},{4,5},{5,6},{6,7},{8,9},{9,10},{10,11},{11... | collective-permute-start | bytes 64520
  68.3 0.0 copy-done
  68.3 0.6 dynamic-slice.4
  69.5 0.0 collective-permute-done
  69.5 0.3 concatenate
  69.8 0.1 copy.7
  70.0 8.5 %all_to_all.19 = bf16[90,8,32]{0,2,1:T(8,128)(2,1)S(1)} all-to-all(bf16[90,8,32]{0,2,1:T(8,128)(2,1)S(1)} %bitcast.10), channel_id=1, replica_groups=mesh['row'=4,'col'=8] {'col'}, dimensions={1} | all-to-all | bytes 92160 | tf_op jit(solution)/shard_map/all_to_all | solution.py:20
  78.5 0.7 all_to_all.17
  (3 shorter events, 0.1 us)
Async XLA Ops:
  6.5 35.7 %all-gather.2.cloned.1.call-start = ((), (), s32[]{:S(2)}) async-start(), calls=%async_computation.1 | async-start | bytes 1884160 | tf_op jit(solution)/shard_map/all_gather | solution.py:9
  7.3 61.0 %copy-start = (u32[32]{0:T(128)S(1)}, u32[32]{0:T(128)}, u32[]{:S(2)}) copy-start(u32[32]{0:T(128)} %constant.3) | copy-start | bytes 388
  67.0 2.6 %collective-permute-start = (bf16[42,256]{1,0:T(8,128)(2,1)S(1)}, bf16[42,256]{1,0:T(8,128)(2,1)S(1)}, u32[]{:S(2)}, u32[]{:S(2)}) collective-permute-start(bf16[42,256]{1,0:T(8,128)(2,1)S(1)} %slice), channel_id=1, source_target_pairs={{0,1},{1,2},{2,3},{3,4},{4,5},{5,6},{6,7},{8,9},{9,10},{10,11},{11... | collective-permute-start | bytes 64520
Sparse Core Ops, SparseCore 0:
  9.2 33.0 all-gather.1
where the time goes:
time: 86.3 us; the launch traced here: 86.1 us
  waiting for transfers between devices  35.7 us (41%)
  blocking collectives  29.2 us (34%)
  between operations  14.1 us (16%)
  matrix products  4 us (5%)
  local copies, waits for them, and re-layouts  1.76 us (2%)
  starting transfers between devices  1.29 us (1%)
    all_gather x1, waiting for transfers between devices, per_device(): gathered = lax.all_gather(amplitudes, 'row', axis=1, tiled=True)  35 us
    unnamed x1, blocking collectives  20.7 us
    all_to_all x1, blocking collectives, per_device(): lax.all_to_all(totals, 'col', split_axis=1, concat_axis=0, tiled=True)  8.52 us
    dot_general x1, matrix products, per_device(): jnp.dot(padded, gathered, preferred_element_type=jnp.float32)  4 us
  transfers between devices with their start and end apart: 2, of which 1 were waited for; matrix products, arithmetic and copies ran while one was open for 1% of the time, Pallas kernels for 0%

commit v1 on v0

--- a/solution.py
+++ b/solution.py
@@ -2,6 +2,17 @@
 import jax.numpy as jnp
 from jax import lax
 from jax.sharding import PartitionSpec as P
+
+
+def in_blocks(value, dim, count):
+    before, after = (value.shape[:dim], value.shape[dim + 1 :])
+    return jnp.moveaxis(value.reshape(*before, count, -1, *after), dim, 0)
+
+
+def laid_out(blocks, dim):
+    blocks = jnp.moveaxis(blocks, 0, dim)
+    shape = blocks.shape
+    return blocks.reshape(*shape[:dim], shape[dim] * shape[dim + 1], *shape[dim + 2 :])
 
 
 def per_device(integrals, amplitudes):
@@ -17,7 +28,14 @@
         scatter_dimension=0,
         tiled=True,
     ).astype(jnp.bfloat16)
-    regrouped = lax.all_to_all(totals, "col", split_axis=1, concat_axis=0, tiled=True)
+    devices, index = (lax.axis_size("col"), lax.axis_index("col"))
+    blocks = in_blocks(totals, 1, devices)
+    done = [blocks[index]]
+    for step in range(1, devices):
+        sent = blocks[index ^ step]
+        done.append(lax.ppermute(sent, "col", [(i, i ^ step) for i in range(devices)]))
+    blocks = jnp.stack(done)[index ^ jnp.arange(devices)]
+    regrouped = laid_out(blocks, 0)
     return regrouped[:local_rows].T
 
 

time: 86.3 us -> 89.3 us (1.035)
  blocking collectives: 29.2 us -> 20.7 us
  starting transfers between devices: 1.29 us -> 9.39 us
  waiting for transfers between devices: 35.7 us -> 38.3 us
    all_to_all x1 -> x0, blocking collectives: 8.52 us -> none  [per_device(): lax.all_to_all(totals, 'col', split_axis=1, concat_axis=0, tiled=True)]
    ppermute x0 -> x7, starting transfers between devices: none -> 8.09 us  [per_device(): lax.ppermute(sent, 'col', [(i, i ^ step) for i in range(devices)])]
    ppermute x0 -> x7, waiting for transfers between devices: none -> 2.7 us  [per_device(): lax.ppermute(sent, 'col', [(i, i ^ step) for i in range(devices)])]
  transfers between devices with their start and end apart: 2 -> 9, of which waited for: 1 -> 3; matrix products, arithmetic and copies ran while one was open for 1% -> 1% of each run, Pallas kernels for 0% -> 0%
where the time goes in v1:
time: 89.3 us; the launch traced here: 89.2 us
  waiting for transfers between devices  38.3 us (43%)
  blocking collectives  20.7 us (23%)
  between operations  14.3 us (16%)
  starting transfers between devices  9.39 us (11%)
  matrix products  4 us (4%)
  local copies, waits for them, and re-layouts  2.41 us (3%)
    all_gather x1, waiting for transfers between devices, per_device(): gathered = lax.all_gather(amplitudes, 'row', axis=1, tiled=True)  34.9 us
    unnamed x1, blocking collectives  20.7 us
    ppermute x7, starting transfers between devices, per_device(): lax.ppermute(sent, 'col', [(i, i ^ step) for i in range(devices)])  8.09 us
    dot_general x1, matrix products, per_device(): jnp.dot(padded, gathered, preferred_element_type=jnp.float32)  4 us
    ppermute x7, waiting for transfers between devices, per_device(): lax.ppermute(sent, 'col', [(i, i ^ step) for i in range(devices)])  2.7 us
  transfers between devices with their start and end apart: 9, of which 3 were waited for; matrix products, arithmetic and copies ran while one was open for 1% of the time, Pallas kernels for 0%

profile of v1, /device:TPU:0, one launch (start us, length us, event | category | flops | bytes accessed | tf_op | source)
XLA Modules:
  0.0 89.2 jit_solution(11442755185314969760)
XLA Ops:
  6.5 0.0 all-gather.2.cloned.1.call-start
  6.5 0.7 all-gather.2.cloned.1.call-update
  7.3 0.0 copy-start
  7.3 34.9 %all-gather.2.cloned.1.call-done = bf16[2880,256]{0,1:T(8,128)(2,1)} async-done(((bf16[2880,64]{0,1:T(8,128)(2,1)}), bf16[2880,256]{0,1:T(8,128)(2,1)}) %all-gather.2.cloned.1.call-update) | async-done | bytes 1474576 | tf_op jit(solution)/shard_map/all_gather | solution.py:20
  42.2 4.0 %fusion.2 = f32[720,256]{1,0:T(8,128)S(1)} fusion(bf16[720,2880]{1,0:T(8,128)(2,1)} %param.2, bf16[2880,256]{0,1:T(8,128)(2,1)} %all-gather.2.cloned.1.call-done), kind=kOutput, calls=%fused_computation.20 | convolution fusion | flops 1061683200 | bytes 6359040 | tf_op jit(solution)/shard_map/dot_general | solution.py:26
  46.2 20.7 %fusion = f32[96,256]{1,0:T(8,128)S(1)} fusion(f32[720,256]{1,0:T(8,128)S(1)} %fusion.2), kind=kCustom, calls=%all-reduce-scatter | all-reduce-scatter fusion | flops 196609 | bytes 836096
  67.0 1.3 %collective-permute-start.7 = (bf16[42,256]{1,0:T(8,128)(2,1)S(1)}, bf16[42,256]{1,0:T(8,128)(2,1)S(1)}, u32[]{:S(2)}, u32[]{:S(2)}) collective-permute-start(bf16[42,256]{1,0:T(8,128)(2,1)S(1)} %slice.2), channel_id=1, source_target_pairs={{0,1},{1,2},{2,3},{3,4},{4,5},{5,6},{6,7},{8,9},{9,10},{10,11},{11... | collective-permute-start | bytes 64520
  68.3 0.0 copy-done
  68.3 0.6 dynamic-slice.36
  69.6 0.0 collective-permute-done.7
  69.6 0.3 concatenate
  69.9 0.1 copy.6
  70.1 0.1 collective-permute-start
  70.2 0.3 collective-permute-start.1
  70.4 1.6 %collective-permute-start.2 = (bf16[90,32]{0,1:T(8,128)(2,1)S(1)}, bf16[90,32]{0,1:T(8,128)(2,1)S(1)}, u32[]{:S(2)}, u32[]{:S(2)}) collective-permute-start(bf16[90,32]{0,1:T(8,128)(2,1)S(1)} %get-tuple-element.9), channel_id=1, source_target_pairs={{0,3},{1,2},{2,1},{3,0},{4,7},{5,6},{6,5},{7,4},{8,11},{9,10},{10,... | collective-permute-start | bytes 17288 | tf_op jit(solution)/shard_map/ppermute | solution.py:36
  72.0 0.6 collective-permute-start.3
  72.6 2.0 %collective-permute-start.4 = (bf16[90,32]{0,1:T(8,128)(2,1)S(1)}, bf16[90,32]{0,1:T(8,128)(2,1)S(1)}, u32[]{:S(2)}, u32[]{:S(2)}) collective-permute-start(bf16[90,32]{0,1:T(8,128)(2,1)S(1)} %get-tuple-element.7), channel_id=1, source_target_pairs={{0,5},{1,4},{2,7},{3,6},{4,1},{5,0},{6,3},{7,2},{8,13},{9,12},{10,... | collective-permute-start | bytes 17288 | tf_op jit(solution)/shard_map/ppermute | solution.py:36
  74.6 0.0 collective-permute-done
  74.6 1.4 %collective-permute-start.5 = (bf16[90,32]{0,1:T(8,128)(2,1)S(1)}, bf16[90,32]{0,1:T(8,128)(2,1)S(1)}, u32[]{:S(2)}, u32[]{:S(2)}) collective-permute-start(bf16[90,32]{0,1:T(8,128)(2,1)S(1)} %get-tuple-element.6), channel_id=1, source_target_pairs={{0,6},{1,7},{2,4},{3,5},{4,2},{5,3},{6,0},{7,1},{8,14},{9,15},{10,... | collective-permute-start | bytes 17288 | tf_op jit(solution)/shard_map/ppermute | solution.py:36
  76.1 0.0 collective-permute-done.1
  76.1 2.1 %collective-permute-start.6 = (bf16[90,32]{0,1:T(8,128)(2,1)S(1)}, bf16[90,32]{0,1:T(8,128)(2,1)S(1)}, u32[]{:S(2)}, u32[]{:S(2)}) collective-permute-start(bf16[90,32]{0,1:T(8,128)(2,1)S(1)} %get-tuple-element.5), channel_id=1, source_target_pairs={{0,7},{1,6},{2,5},{3,4},{4,3},{5,2},{6,1},{7,0},{8,15},{9,14},{10,... | collective-permute-start | bytes 17288 | tf_op jit(solution)/shard_map/ppermute | solution.py:36
  78.2 0.0 collective-permute-done.2
  78.2 0.0 collective-permute-done.3
  78.2 0.0 collective-permute-done.4
  78.3 1.8 %collective-permute-done.5 = bf16[90,32]{0,1:T(8,128)(2,1)S(1)} collective-permute-done((bf16[90,32]{0,1:T(8,128)(2,1)S(1)}, bf16[90,32]{0,1:T(8,128)(2,1)S(1)}, u32[]{:S(2)}, u32[]{:S(2)}) %collective-permute-start.5) | collective-permute-done | bytes 5792 | tf_op jit(solution)/shard_map/ppermute | solution.py:36
  80.1 0.9 collective-permute-done.6
  81.0 0.6 gather_fusion
  81.6 0.7 reshape.38
  (14 shorter events, 0.2 us)
Async XLA Ops:
  6.5 35.7 %all-gather.2.cloned.1.call-start = ((), (), s32[]{:S(2)}) async-start(), calls=%async_computation | async-start | bytes 1884160 | tf_op jit(solution)/shard_map/all_gather | solution.py:20
  7.3 61.1 %copy-start = (u32[32]{0:T(128)S(1)}, u32[32]{0:T(128)}, u32[]{:S(2)}) copy-start(u32[32]{0:T(128)} %constant.26) | copy-start | bytes 388
  67.0 2.6 %collective-permute-start.7 = (bf16[42,256]{1,0:T(8,128)(2,1)S(1)}, bf16[42,256]{1,0:T(8,128)(2,1)S(1)}, u32[]{:S(2)}, u32[]{:S(2)}) collective-permute-start(bf16[42,256]{1,0:T(8,128)(2,1)S(1)} %slice.2), channel_id=1, source_target_pairs={{0,1},{1,2},{2,3},{3,4},{4,5},{5,6},{6,7},{8,9},{9,10},{10,11},{11... | collective-permute-start | bytes 64520
  70.1 4.6 %collective-permute-start = (bf16[90,32]{0,1:T(8,128)(2,1)S(1)}, bf16[90,32]{0,1:T(8,128)(2,1)S(1)}, u32[]{:S(2)}, u32[]{:S(2)}) collective-permute-start(bf16[90,32]{0,1:T(8,128)(2,1)S(1)} %get-tuple-element.11), channel_id=1, source_target_pairs={{0,1},{1,0},{2,3},{3,2},{4,5},{5,4},{6,7},{7,6},{8,9},{9,8},{10,11... | collective-permute-start | bytes 17288 | tf_op jit(solution)/shard_map/ppermute | solution.py:36
  70.2 5.9 %collective-permute-start.1 = (bf16[90,32]{0,1:T(8,128)(2,1)S(1)}, bf16[90,32]{0,1:T(8,128)(2,1)S(1)}, u32[]{:S(2)}, u32[]{:S(2)}) collective-permute-start(bf16[90,32]{0,1:T(8,128)(2,1)S(1)} %get-tuple-element.10), channel_id=1, source_target_pairs={{0,2},{1,3},{2,0},{3,1},{4,6},{5,7},{6,4},{7,5},{8,10},{9,11},{10,... | collective-permute-start | bytes 17288 | tf_op jit(solution)/shard_map/ppermute | solution.py:36
  70.4 7.8 %collective-permute-start.2 = (bf16[90,32]{0,1:T(8,128)(2,1)S(1)}, bf16[90,32]{0,1:T(8,128)(2,1)S(1)}, u32[]{:S(2)}, u32[]{:S(2)}) collective-permute-start(bf16[90,32]{0,1:T(8,128)(2,1)S(1)} %get-tuple-element.9), channel_id=1, source_target_pairs={{0,3},{1,2},{2,1},{3,0},{4,7},{5,6},{6,5},{7,4},{8,11},{9,10},{10,... | collective-permute-start | bytes 17288 | tf_op jit(solution)/shard_map/ppermute | solution.py:36
  72.0 6.2 %collective-permute-start.3 = (bf16[90,32]{0,1:T(8,128)(2,1)S(1)}, bf16[90,32]{0,1:T(8,128)(2,1)S(1)}, u32[]{:S(2)}, u32[]{:S(2)}) collective-permute-start(bf16[90,32]{0,1:T(8,128)(2,1)S(1)} %get-tuple-element.8), channel_id=1, source_target_pairs={{0,4},{1,5},{2,6},{3,7},{4,0},{5,1},{6,2},{7,3},{8,12},{9,13},{10,... | collective-permute-start | bytes 17288 | tf_op jit(solution)/shard_map/ppermute | solution.py:36
  72.6 5.6 %collective-permute-start.4 = (bf16[90,32]{0,1:T(8,128)(2,1)S(1)}, bf16[90,32]{0,1:T(8,128)(2,1)S(1)}, u32[]{:S(2)}, u32[]{:S(2)}) collective-permute-start(bf16[90,32]{0,1:T(8,128)(2,1)S(1)} %get-tuple-element.7), channel_id=1, source_target_pairs={{0,5},{1,4},{2,7},{3,6},{4,1},{5,0},{6,3},{7,2},{8,13},{9,12},{10,... | collective-permute-start | bytes 17288 | tf_op jit(solution)/shard_map/ppermute | solution.py:36
  74.6 5.4 %collective-permute-start.5 = (bf16[90,32]{0,1:T(8,128)(2,1)S(1)}, bf16[90,32]{0,1:T(8,128)(2,1)S(1)}, u32[]{:S(2)}, u32[]{:S(2)}) collective-permute-start(bf16[90,32]{0,1:T(8,128)(2,1)S(1)} %get-tuple-element.6), channel_id=1, source_target_pairs={{0,6},{1,7},{2,4},{3,5},{4,2},{5,3},{6,0},{7,1},{8,14},{9,15},{10,... | collective-permute-start | bytes 17288 | tf_op jit(solution)/shard_map/ppermute | solution.py:36
  76.1 4.9 %collective-permute-start.6 = (bf16[90,32]{0,1:T(8,128)(2,1)S(1)}, bf16[90,32]{0,1:T(8,128)(2,1)S(1)}, u32[]{:S(2)}, u32[]{:S(2)}) collective-permute-start(bf16[90,32]{0,1:T(8,128)(2,1)S(1)} %get-tuple-element.5), channel_id=1, source_target_pairs={{0,7},{1,6},{2,5},{3,4},{4,3},{5,2},{6,1},{7,0},{8,15},{9,14},{10,... | collective-permute-start | bytes 17288 | tf_op jit(solution)/shard_map/ppermute | solution.py:36
Sparse Core Ops, SparseCore 0:
  9.2 33.0 all-gather.1
